TPU v7x, 1024 devices: a whole 4x8x16 slice. The times are simulated.
1024 devices in a mesh: dp: 32 (over z, core), group: 4 (over x), tensor: 8 (over y).
Axes of the slice: x: 4, y: 8, z: 16, core: 2. Of those that a mesh axis runs over, the one named last changes fastest.
Arguments:
- attn_heads: bfloat16 [8192, 8192], P('dp', ('group', 'tensor')), parts along dimension 0, may hold values from -6 to 6
- out_proj: bfloat16 [8192, 3584], P(('group', 'tensor')), may hold values from -0.0625 to 0.0625
- residual_in: bfloat16 [8192, 3584], P(('dp', 'group', 'tensor')), parts along dimension 0, may hold values from -6 to 6
- norm_gain: float32 [3584], replicated, may hold values from 0.1 to 1.9
- expert_ids: int32 [8192, 4], P(('dp', 'group', 'tensor')), parts along dimension 0, may hold values from 0 to 7, as said below
- gate_weights: bfloat16 [8192, 4], P(('dp', 'group', 'tensor')), parts along dimension 0, may hold values from 0.19921875 to 1.5
- w_gate: bfloat16 [8, 3584, 1024], P('group', None, 'tensor'), may hold values from -0.09375 to 0.09375
- w_up: bfloat16 [8, 3584, 1024], P('group', None, 'tensor'), may hold values from -0.09375 to 0.09375
- w_down: bfloat16 [8, 1024, 3584], P('group', 'tensor'), may hold values from -0.1875 to 0.1875
Outputs:
- layer_out: bfloat16 [8192, 3584], P(('dp', 'group', 'tensor')), parts along dimension 0
There are 32 independent parts, one for each index of `dp`. A program takes and returns all parts, laid end to end along the dimension named above; an argument that names none is the same for every part. Nothing has to cross between parts.
Inputs may be any that keep to these rules, and one draw needn't show every extreme that they name: `expert_ids`: each row names 4 different experts, of at most 3 node groups (expert e belongs to node group e // 2). In each aligned block of 8 rows (the rows of one device) at most 6 rows name experts of any one node group, and in every draw some node group is named by exactly 6 rows of every block.
All inputs are finite; a program needn't handle non-finite values.
Results may differ from a plain program's by a relative error of at most 0.02.
Values may be sent and summed in bfloat16 or wider, within the bound.
No kernel may reach another device: no remote copies, remote signals or barrier semaphores. Data moves between devices by JAX's collectives and lax.ppermute only.
A program may use at most 64 MiB of HBM per device.

v0:
```python
import jax
import jax.numpy as jnp
from jax import lax
from jax.sharding import PartitionSpec as P


def own_rows(terms, axes):
    so_far = terms.astype(jnp.bfloat16)
    for axis in axes:
        so_far = lax.psum_scatter(so_far, axis, scatter_dimension=0, tiled=True)
    return so_far.astype(jnp.float32)


def sent_to_all(shard, axis):
    count = lax.axis_size(axis)
    return lax.all_to_all(
        jnp.broadcast_to(shard[None], (count, *shard.shape)), axis, 0, 0, tiled=True
    )


def in_order(tiles, dim):
    shape = list(tiles.shape[1:])
    shape[dim] *= tiles.shape[0]
    return jnp.moveaxis(tiles, 0, dim).reshape(shape)


def gather_directly(shard, axis, dim):
    tiles = sent_to_all(shard, axis)
    return in_order(tiles, dim)


def sent_together(arrays, axis, dim, along):
    both = jnp.concatenate(arrays, axis=along)
    filled, at, done = (gather_directly(both, axis, dim), 0, [])
    for a in arrays:
        done.append(lax.slice_in_dim(filled, at, at + a.shape[along], axis=along))
        at += a.shape[along]
    return tuple(done)


def in_blocks(shard, dim, count):
    shape = shard.shape
    tiles = shard.reshape(*shape[:dim], count, shape[dim] // count, *shape[dim + 1 :])
    return jnp.moveaxis(tiles, dim, 0)


def summed_on_arrival(shard, axis, dim):
    count = lax.axis_size(axis)
    tiles = lax.all_to_all(in_blocks(shard, dim, count), axis, 0, 0, tiled=True)
    return jnp.sum(tiles.astype(jnp.float32), axis=0)


def slot_tables(table, groups, members, capacity):
    node_weights = table.astype(jnp.float32).reshape(table.shape[:-1] + (groups, members))
    chosen = (jnp.sum(node_weights, axis=-1) > 0).astype(jnp.float32)
    position = jnp.cumsum(chosen, axis=-2) - 1.0
    slot_ids = jnp.arange(capacity, dtype=jnp.float32)
    slot_map = chosen[..., None] * (position[..., None] == slot_ids).astype(jnp.float32)
    return (slot_map, node_weights)


def on_device(
    attn_heads, out_proj, residual_in, norm_gain, expert_ids, gate_weights, w_gate, w_up, w_down
):
    tokens_here = residual_in.shape[0]
    features = residual_in.shape[1]
    groups = lax.axis_size("group")
    tensors = lax.axis_size("tensor")
    members = w_gate.shape[0]
    experts_all = groups * members
    capacity = 3 * tokens_here // 4
    projected = own_rows(
        jnp.dot(attn_heads, out_proj, preferred_element_type=jnp.float32), ("group", "tensor")
    ).astype(jnp.bfloat16)
    hidden = (residual_in.astype(jnp.float32) + projected.astype(jnp.float32)).astype(jnp.bfloat16)
    stream = hidden.astype(jnp.float32)
    scale = lax.rsqrt(jnp.mean(stream * stream, axis=1, keepdims=True) + 1e-06)
    normed = (stream * scale * norm_gain).astype(jnp.bfloat16)
    matches = (
        expert_ids[:, :, None] == jnp.arange(experts_all, dtype=jnp.int32)[None, None, :]
    ).astype(jnp.float32)
    table = jnp.sum(matches * gate_weights.astype(jnp.float32)[:, :, None], axis=1).astype(
        jnp.bfloat16
    )
    slot_map, node_weights = slot_tables(table, groups, members, capacity)
    slot_bf = slot_map.astype(jnp.bfloat16)
    seen_rows, seen_table = sent_together((normed, table), "tensor", 0, 1)
    seen_rows = seen_rows.reshape(tensors, tokens_here, features)
    seen_table = seen_table.reshape(tensors, tokens_here, experts_all)
    slot_all, weights_source = slot_tables(seen_table, groups, members, capacity)
    send_rows = jnp.einsum(
        "trgc,trd->gtcd",
        slot_all.astype(jnp.bfloat16),
        seen_rows,
        preferred_element_type=jnp.float32,
    ).astype(jnp.bfloat16)
    send_weights = jnp.einsum("trgc,trgj->gtcj", slot_all, weights_source).astype(jnp.bfloat16)
    rows_all, weights_all = (
        lax.all_to_all(send_rows, "group", split_axis=0, concat_axis=0, tiled=True),
        lax.all_to_all(send_weights, "group", split_axis=0, concat_axis=0, tiled=True),
    )
    received = rows_all.reshape(-1, features)
    expert_weights = weights_all.reshape(-1, members).astype(jnp.float32)
    summed = jnp.zeros((received.shape[0], features), jnp.float32)
    for member in range(members):
        gate_proj = jnp.dot(received, w_gate[member], preferred_element_type=jnp.float32)
        up_proj = jnp.dot(received, w_up[member], preferred_element_type=jnp.float32)
        activated = (jax.nn.silu(gate_proj) * up_proj).astype(jnp.bfloat16)
        summed = summed + expert_weights[:, member : member + 1] * jnp.dot(
            activated, w_down[member], preferred_element_type=jnp.float32
        )
    partial_value = summed.reshape(groups, tensors, capacity, features)
    folded = summed_on_arrival(partial_value.astype(jnp.bfloat16), "tensor", 1)
    folded = folded.astype(jnp.bfloat16).reshape(groups, capacity, features)
    node_rows = lax.all_to_all(folded, "group", split_axis=0, concat_axis=0, tiled=True)
    mixture = jnp.einsum("rgc,gcd->rd", slot_bf, node_rows, preferred_element_type=jnp.float32)
    return (stream + mixture).astype(jnp.bfloat16)


def solution(mesh):
    placed = (
        P("dp", ("group", "tensor")),
        P(("group", "tensor"), None),
        P(("dp", "group", "tensor"), None),
        P(),
        P(("dp", "group", "tensor"), None),
        P(("dp", "group", "tensor"), None),
        P("group", None, "tensor"),
        P("group", None, "tensor"),
        P("group", "tensor", None),
    )
    return jax.shard_map(
        on_device,
        mesh=mesh,
        in_specs=placed,
        out_specs=P(("dp", "group", "tensor"), None),
        check_vma=False,
    )
```

profile of v0, /device:TPU:64, one launch (start us, length us, event | category | flops | bytes accessed | tf_op | source)
XLA Modules:
  0.0 223.5 jit_solution(2824006635790815820)
XLA Ops:
  6.5 1.5 copy-done
  8.0 2.8 %convolution_convert_fusion.1 = bf16[256,3584]{1,0:T(8,128)(2,1)} fusion(bf16[256,256]{1,0:T(8,128)(2,1)} %param.9, bf16[256,3584]{1,0:T(8,128)(2,1)S(1)} %copy-done), kind=kOutput, calls=%fused_computation.4 | convolution fusion | flops 470679552 | bytes 3801088 | tf_op jit(solution)/shard_map/dot_general | solution.py:73
  10.9 45.4 %reduce-scatter.3.cloned.1.call-done = bf16[64,3584]{1,0:T(8,128)(2,1)} async-done(((bf16[256,3584]{1,0:T(8,128)(2,1)}), bf16[64,3584]{1,0:T(8,128)(2,1)}) %reduce-scatter.3.cloned.1.call-update) | async-done | bytes 458768 | tf_op jit(solution)/shard_map/reduce_scatter | solution.py:10
  56.4 48.5 %reduce-scatter.5.cloned.1.call-done = bf16[8,3584]{1,0:T(8,128)(2,1)} async-done(((bf16[64,3584]{1,0:T(8,128)(2,1)}), bf16[8,3584]{1,0:T(8,128)(2,1)}) %reduce-scatter.5.cloned.1.call-update) | async-done | bytes 57360 | tf_op jit(solution)/shard_map/reduce_scatter | solution.py:10
  104.9 1.0 fusion.27
  105.9 0.9 fusion.29
  106.9 17.0 %all_to_all.25 = bf16[8,8,3592]{2,1,0:T(8,128)(2,1)S(1)} all-to-all(bf16[8,8,3592]{2,1,0:T(8,128)(2,1)S(1)} %broadcast_in_dim.2), channel_id=1, replica_groups=mesh['dp'=32,'group'=4,'tensor'=8] {'tensor'}, dimensions={0} | all-to-all | bytes 919552 | tf_op jit(solution)/shard_map/all_to_all | solution.py:16
  124.1 0.7 reduce_window_sum.23
  124.8 0.2 convolution_convert_fusion.2
  125.0 0.7 copy.76
  125.7 4.2 %all-to-all-start.1 = ((bf16[4,8,6,2]{1,3,2,0:T(2,128)(2,1)}), bf16[4,8,6,2]{1,3,2,0:T(2,128)(2,1)S(1)}, u32[]{:S(2)}, u32[]{:S(2)}) async-start(bf16[4,8,6,2]{1,3,2,0:T(2,128)(2,1)} %copy.76), calls=%async_computation.3 | async-start | bytes 24576 | tf_op jit(solution)/shard_map/all_to_all | solution.py:100
  130.0 0.6 fusion.2
  130.6 1.8 copy.79
  132.4 2.9 %all-to-all-done.1 = bf16[4,8,6,2]{1,3,2,0:T(2,128)(2,1)S(1)} async-done(((bf16[4,8,6,2]{1,3,2,0:T(2,128)(2,1)}), bf16[4,8,6,2]{1,3,2,0:T(2,128)(2,1)S(1)}, u32[]{:S(2)}, u32[]{:S(2)}) %all-to-all-start.1) | async-done | bytes 800 | tf_op jit(solution)/shard_map/all_to_all | solution.py:100
  135.3 3.5 %all-to-all-start.2 = ((bf16[4,8,6,3584]{3,1,2,0:T(8,128)(2,1)}), bf16[4,8,6,3584]{3,1,2,0:T(8,128)(2,1)S(1)}, u32[]{:S(2)}, u32[]{:S(2)}) async-start(bf16[4,8,6,3584]{3,1,2,0:T(8,128)(2,1)} %copy.79), calls=%async_computation.4 | async-start | bytes 2752512 | tf_op jit(solution)/shard_map/all_to_all | solution.py:99
  139.1 12.4 %all-to-all-done.2 = bf16[4,8,6,3584]{3,1,2,0:T(8,128)(2,1)S(1)} async-done(((bf16[4,8,6,3584]{3,1,2,0:T(8,128)(2,1)}), bf16[4,8,6,3584]{3,1,2,0:T(8,128)(2,1)S(1)}, u32[]{:S(2)}, u32[]{:S(2)}) %all-to-all-start.2) | async-done | bytes 1376288 | tf_op jit(solution)/shard_map/all_to_all | solution.py:99
  151.5 1.7 copy.80
  153.1 2.4 %reshape.82 = bf16[192,3584]{1,0:T(8,128)(2,1)S(1)} reshape(bf16[4,8,6,3584]{3,2,1,0:T(8,128)(2,1)} %copy.80) | data formatting | bytes 2752512 | tf_op jit(solution)/shard_map/reshape | solution.py:102
  155.6 1.8 fusion.15
  157.4 0.5 fusion.10
  157.9 4.0 %convolution_multiply_fusion.1 = f32[192,3584]{1,0:T(8,128)} fusion(f32[192]{0:T(256)S(1)} %bitcast.57, bf16[192,3584]{1,0:T(8,128)(2,1)S(1)} %reshape.82, bf16[2,128,3584]{2,1,0:T(8,128)(2,1)} %param.17, bf16[2,3584,128]{2,1,0:T(8,128)(2,1)} %param.16, f32[192,128]{1,0:T(8,128)S(1)} %fusion.15), kind=kOutput, calls=%fused_computation.2 | convolution fusion | flops 353157120 | bytes 6062848 | tf_op jit(solution)/shard_map/dot_general | solution.py:109
  161.9 4.4 %fusion.1 = bf16[192,3584]{1,0:T(8,128)(2,1)} fusion(f32[192,3584]{1,0:T(8,128)} %convolution_multiply_fusion.1, f32[192]{0:T(256)S(1)} %bitcast.58, bf16[192,3584]{1,0:T(8,128)(2,1)S(1)} %reshape.82, bf16[2,128,3584]{2,1,0:T(8,128)(2,1)} %param.17, bf16[2,3584,128]{2,1,0:T(8,128)(2,1)} %param.16, f32[192,128]{1,0:T(8,128)S(1)} %fusion.10), kind=kOutput, calls=%fused_computation.5 | convolution fusion | flops 354533376 | bytes 7439104 | tf_op jit(solution)/shard_map/dot_general | solution.py:109
  166.3 3.4 %convert_element_type.132 = bf16[4,8,1,6,3584]{4,3,1,0,2:T(8,128)(2,1)} reshape(bf16[192,3584]{1,0:T(8,128)(2,1)} %fusion.1) | data formatting | bytes 2752512 | tf_op jit(solution)/shard_map/convert_element_type | solution.py:113
  169.7 3.7 %copy.81 = bf16[8,4,1,6,3584]{4,1,3,2,0:T(4,128)(2,1)} copy(bf16[8,4,1,6,3584]{4,3,0,1,2:T(8,128)(2,1)} %bitcast.53) | data formatting | bytes 2752512 | tf_op jit(solution)/shard_map/transpose | solution.py:44
  173.4 3.6 %all-to-all-start.3 = ((bf16[8,4,1,6,3584]{4,1,3,2,0:T(4,128)(2,1)}), bf16[8,4,1,6,3584]{4,1,3,2,0:T(4,128)(2,1)S(1)}, u32[]{:S(2)}, u32[]{:S(2)}) async-start(bf16[8,4,1,6,3584]{4,1,3,2,0:T(4,128)(2,1)} %copy.81), calls=%async_computation.5 | async-start | bytes 2752512 | tf_op jit(solution)/shard_map/all_to_all | solution.py:49
  177.0 0.2 reduce_window_sum.22
  177.2 27.1 %all-to-all-done.3 = bf16[8,4,1,6,3584]{4,1,3,2,0:T(4,128)(2,1)S(1)} async-done(((bf16[8,4,1,6,3584]{4,1,3,2,0:T(4,128)(2,1)}), bf16[8,4,1,6,3584]{4,1,3,2,0:T(4,128)(2,1)S(1)}, u32[]{:S(2)}, u32[]{:S(2)}) %all-to-all-start.3) | async-done | bytes 1376288 | tf_op jit(solution)/shard_map/all_to_all | solution.py:49
  204.3 0.7 reduce_sum.52
  205.1 0.7 copy.82
  205.8 3.4 %all-to-all-start.4 = ((bf16[4,6,3584]{2,1,0:T(8,128)(2,1)}), bf16[4,6,3584]{2,1,0:T(8,128)(2,1)S(1)}, u32[]{:S(2)}, u32[]{:S(2)}) async-start(bf16[4,6,3584]{2,1,0:T(8,128)(2,1)} %copy.82), calls=%async_computation.6 | async-start | bytes 458752 | tf_op jit(solution)/shard_map/all_to_all | solution.py:115
  209.2 6.5 %all-to-all-done.4 = bf16[4,6,3584]{2,1,0:T(8,128)(2,1)S(1)} async-done(((bf16[4,6,3584]{2,1,0:T(8,128)(2,1)}), bf16[4,6,3584]{2,1,0:T(8,128)(2,1)S(1)}, u32[]{:S(2)}, u32[]{:S(2)}) %all-to-all-start.4) | async-done | bytes 172064 | tf_op jit(solution)/shard_map/all_to_all | solution.py:115
  215.7 1.0 fusion.4
  (38 shorter events, 0.8 us)
Async XLA Ops:
  6.5 1.5 copy-start
  6.5 49.8 %reduce-scatter.3.cloned.1.call-start = ((), (), s32[]{:S(2)}) async-start(), calls=%async_computation.7 | async-start | bytes 2293760 | tf_op jit(solution)/shard_map/reduce_scatter | solution.py:10
  10.8 45.5 %copy-start.5 = (bf16[8,4]{0,1:T(4,128)(2,1)S(1)}, bf16[8,4]{0,1:T(4,128)(2,1)}, u32[]{:S(2)}) copy-start(bf16[8,4]{0,1:T(4,128)(2,1)} %param.14) | copy-start | bytes 196
  10.8 45.5 %copy-start.4 = (s32[8,4]{0,1:T(4,128)S(1)}, s32[8,4]{0,1:T(4,128)}, u32[]{:S(2)}) copy-start(s32[8,4]{0,1:T(4,128)} %param.13) | copy-start | bytes 388
  10.8 94.1 %copy-start.1 = (bf16[8,3584]{1,0:T(8,128)(2,1)S(1)}, bf16[8,3584]{1,0:T(8,128)(2,1)}, u32[]{:S(2)}) copy-start(bf16[8,3584]{1,0:T(8,128)(2,1)} %param.11) | copy-start | bytes 172036
  10.8 95.1 %copy-start.3 = (f32[3584]{0:T(1024)S(1)}, f32[3584]{0:T(1024)}, u32[]{:S(2)}) copy-start(f32[3584]{0:T(1024)} %param.12) | copy-start | bytes 43012
  10.9 94.1 %reduce-scatter.5.cloned.1.call-start = ((), (), s32[]{:S(2)}) async-start(), calls=%async_computation.8 | async-start | bytes 516096 | tf_op jit(solution)/shard_map/reduce_scatter | solution.py:10
  125.7 9.6 %all-to-all-start.1 = ((bf16[4,8,6,2]{1,3,2,0:T(2,128)(2,1)}), bf16[4,8,6,2]{1,3,2,0:T(2,128)(2,1)S(1)}, u32[]{:S(2)}, u32[]{:S(2)}) async-start(bf16[4,8,6,2]{1,3,2,0:T(2,128)(2,1)} %copy.76), calls=%async_computation.3 | async-start | bytes 24576 | tf_op jit(solution)/shard_map/all_to_all | solution.py:100
  135.3 16.2 %all-to-all-start.2 = ((bf16[4,8,6,3584]{3,1,2,0:T(8,128)(2,1)}), bf16[4,8,6,3584]{3,1,2,0:T(8,128)(2,1)S(1)}, u32[]{:S(2)}, u32[]{:S(2)}) async-start(bf16[4,8,6,3584]{3,1,2,0:T(8,128)(2,1)} %copy.79), calls=%async_computation.4 | async-start | bytes 2752512 | tf_op jit(solution)/shard_map/all_to_all | solution.py:99
  155.6 1.8 copy-start.6
  173.4 31.0 %all-to-all-start.3 = ((bf16[8,4,1,6,3584]{4,1,3,2,0:T(4,128)(2,1)}), bf16[8,4,1,6,3584]{4,1,3,2,0:T(4,128)(2,1)S(1)}, u32[]{:S(2)}, u32[]{:S(2)}) async-start(bf16[8,4,1,6,3584]{4,1,3,2,0:T(4,128)(2,1)} %copy.81), calls=%async_computation.5 | async-start | bytes 2752512 | tf_op jit(solution)/shard_map/all_to_all | solution.py:49
  176.9 38.7 %copy-start.2 = (bf16[8,3584]{1,0:T(8,128)(2,1)S(1)}, bf16[8,3584]{1,0:T(8,128)(2,1)}, u32[]{:S(2)}) copy-start(bf16[8,3584]{1,0:T(8,128)(2,1)} %reduce-scatter.5.cloned.1.call-done) | copy-start | bytes 172036
  205.8 9.9 %all-to-all-start.4 = ((bf16[4,6,3584]{2,1,0:T(8,128)(2,1)}), bf16[4,6,3584]{2,1,0:T(8,128)(2,1)S(1)}, u32[]{:S(2)}, u32[]{:S(2)}) async-start(bf16[4,6,3584]{2,1,0:T(8,128)(2,1)} %copy.82), calls=%async_computation.6 | async-start | bytes 458752 | tf_op jit(solution)/shard_map/all_to_all | solution.py:115
Sparse Core Ops, SparseCore 0:
  11.0 45.2 reduce-scatter.2
  59.7 45.1 reduce-scatter.4
where the time goes:
time: 224 us; the launch traced here: 223 us
  waiting for transfers between devices  143 us (64%)
  blocking collectives  17 us (8%)
  local copies, waits for them, and re-layouts  16.5 us (7%)
  matrix products  15.2 us (7%)
  starting transfers between devices  14.8 us (7%)
  between operations  13.6 us (6%)
  other arithmetic  3.6 us (2%)
    reduce_scatter x2, waiting for transfers between devices, own_rows(): so_far = lax.psum_scatter(so_far, axis, scatter_dimension=0, tiled=True)  93.9 us
    all_to_all x1, waiting for transfers between devices, summed_on_arrival(): tiles = lax.all_to_all(in_blocks(shard, dim, count), axis, 0, 0, tiled=True)  27.1 us
    all_to_all x1, blocking collectives, sent_to_all(): lax.all_to_all(jnp.broadcast_to(shard[None], (count, *shard.shape)), axis...  17 us
    all_to_all x1, waiting for transfers between devices, on_device(): lax.all_to_all(send_rows, 'group', split_axis=0, concat_axis=0, tiled=True)  12.4 us
    dot_general x2, matrix products, on_device(): jnp.dot(activated, w_down[member], preferred_element_type=jnp.float32)  8.35 us
    all_to_all x1, waiting for transfers between devices, on_device(): lax.all_to_all(folded, 'group', split_axis=0, concat_axis=0, tiled=True)  6.46 us
  transfers between devices with their start and end apart: 6, of which 6 were waited for; matrix products, arithmetic and copies ran while one was open for 1% of the time, Pallas kernels for 0%

commit v1 on v0

v1 whole, which is shorter than its diff:
```python
import jax
import jax.numpy as jnp
from jax import lax
from jax.experimental import pallas as pl
from jax.experimental.pallas import tpu as pltpu
from jax.sharding import Mesh, PartitionSpec as P

BF = jnp.bfloat16
F32 = jnp.float32
LANES = 128


def whole(shape):
    return pl.BlockSpec(shape, lambda *_: (0,) * len(shape))


def call(body, outs, grid=None, in_specs=None, out_specs=None, scratch=(), vmem=20 << 20):
    return pl.pallas_call(
        body,
        out_shape=outs,
        grid=grid if grid is not None else (),
        in_specs=in_specs,
        out_specs=out_specs,
        scratch_shapes=scratch,
        compiler_params=pltpu.CompilerParams(vmem_limit_bytes=vmem),
    )


def exchange(blocks, axes):
    return lax.all_to_all(blocks, axes, 0, 0, tiled=True)


def project(attn, weight, groups, quads, pairs, tokens):
    rows, depth = attn.shape
    features = weight.shape[1]
    width = 512

    def body(a_ref, w_ref, o_ref):
        out = jnp.dot(a_ref[...], w_ref[...], preferred_element_type=F32).astype(BF)
        for g in range(groups):
            for p in range(pairs):
                for q in range(quads):
                    src = ((g * quads + q) * pairs + p) * tokens
                    dst = ((g * pairs + p) * quads + q) * tokens
                    o_ref[dst : dst + tokens, :] = out[src : src + tokens, :]

    return call(
        body,
        jax.ShapeDtypeStruct((rows, features), BF),
        grid=(features // width,),
        in_specs=[whole((rows, depth)), pl.BlockSpec((depth, width), lambda j: (0, j))],
        out_specs=pl.BlockSpec((rows, width), lambda j: (0, j)),
    )(attn, weight)


def sum_blocks(blocks):
    count, rows, features = blocks.shape

    def body(x_ref, o_ref):
        total = x_ref[0].astype(F32)
        for s in range(1, count):
            total = total + x_ref[s].astype(F32)
        o_ref[...] = total.astype(BF)

    return call(
        body,
        jax.ShapeDtypeStruct((rows, features), BF),
        in_specs=[pl.BlockSpec(memory_space=pltpu.VMEM)],
        out_specs=pl.BlockSpec(memory_space=pltpu.VMEM),
    )(blocks)


def finish_hidden(parts, residual, gain, ids, gates, copies, experts):
    count, tokens, features = parts.shape

    def body(x_ref, r_ref, g_ref, id_ref, w_ref, h_ref, o_ref):
        total = x_ref[0].astype(F32)
        for s in range(1, count):
            total = total + x_ref[s].astype(F32)
        projected = total.astype(BF).astype(F32)
        hidden = (r_ref[...].astype(F32) + projected).astype(BF)
        h_ref[...] = hidden
        stream = hidden.astype(F32)
        scale = lax.rsqrt(jnp.mean(stream * stream, axis=1, keepdims=True) + 1e-06)
        normed = (stream * scale * g_ref[...]).astype(BF)
        lane = lax.broadcasted_iota(jnp.int32, (tokens, LANES), 1)
        table = jnp.zeros((tokens, LANES), F32)
        picks = id_ref[...]
        gate = w_ref[...].astype(F32)
        for k in range(picks.shape[1]):
            table = table + jnp.where(lane == picks[:, k : k + 1], gate[:, k : k + 1], 0.0)
        table = table.astype(BF)
        for s in range(copies):
            o_ref[s, :, :features] = normed
            o_ref[s, :, features:] = table

    return call(
        body,
        (
            jax.ShapeDtypeStruct((tokens, features), BF),
            jax.ShapeDtypeStruct((copies, tokens, features + LANES), BF),
        ),
        in_specs=[pl.BlockSpec(memory_space=pltpu.VMEM)] * 5,
        out_specs=(pl.BlockSpec(memory_space=pltpu.VMEM),) * 2,
    )(parts, residual, gain, ids, gates)


def slot_of(index, slots):
    block = (index * 171) >> 10 if slots == 6 else index // slots
    return block, index - block * slots


def one_hot(table, table_first, groups, quads, repeat, tokens, slots):
    here = quads * tokens
    there = groups * repeat * quads * slots
    members = 2

    def split(index):
        block, slot = slot_of(index, slots)
        quad = block % quads
        group = block // (quads * repeat)
        return group, quad, slot

    group_e, _, _ = split(lax.broadcasted_iota(jnp.int32, (there, LANES), 0))
    expert = lax.broadcasted_iota(jnp.int32, (there, LANES), 1)
    belongs = (expert // members == group_e).astype(BF)
    shape = (here, there) if table_first else (there, here)
    t_dim, s_dim = (0, 1) if table_first else (1, 0)
    nt = (((1,), (1,)), ((), ()))
    pair = (table, belongs) if table_first else (belongs, table)
    chosen = lax.dot_general(*pair, nt, preferred_element_type=F32) > 0
    chosen = jnp.where(chosen, 1.0, 0.0)
    a = lax.broadcasted_iota(jnp.int32, (here, here), 0)
    b = lax.broadcasted_iota(jnp.int32, (here, here), 1)
    row, col = (a, b) if table_first else (b, a)
    before = jnp.where((row // tokens == col // tokens) & (col < row), 1.0, 0.0).astype(BF)
    flag = chosen.astype(BF)
    if table_first:
        position = jnp.dot(before, flag, preferred_element_type=F32)
    else:
        position = jnp.dot(flag, before, preferred_element_type=F32)
    _, quad, slot = split(lax.broadcasted_iota(jnp.int32, shape, s_dim))
    token = lax.broadcasted_iota(jnp.int32, shape, t_dim)
    hit = (token // tokens == quad) & (position == slot.astype(F32))
    return jnp.where(hit, chosen, 0.0).astype(BF)


def pick_rows(seen, groups, quads, pairs, tokens, slots):
    here, wide = seen.shape
    features = wide - LANES
    span = quads * slots

    def body(x_ref, o_ref, t_ref):
        table = x_ref[:, features:]
        t_ref[...] = table
        hot = one_hot(table, False, groups, quads, 1, tokens, slots)
        picked = jnp.dot(hot, x_ref[...], preferred_element_type=F32).astype(BF)
        for g in range(groups):
            for p in range(pairs):
                at = (g * pairs + p) * span
                o_ref[at : at + span, :] = picked[g * span : (g + 1) * span, :]

    return call(
        body,
        (
            jax.ShapeDtypeStruct((groups * pairs * span, wide), BF),
            jax.ShapeDtypeStruct((here, LANES), BF),
        ),
        in_specs=[pl.BlockSpec(memory_space=pltpu.VMEM)],
        out_specs=(pl.BlockSpec(memory_space=pltpu.VMEM),) * 2,
    )(seen)


def experts_of(rows, w_gate, w_up, w_down, group):
    count, wide = rows.shape
    features = wide - LANES
    members, _, units = w_gate.shape

    def body(g_ref, x_ref, wg_ref, wu_ref, wd_ref, o_ref):
        table = x_ref[:, features:].astype(F32)
        lane = lax.broadcasted_iota(jnp.int32, (count, LANES), 1)
        x = x_ref[:, :features]
        acts = []
        for m in range(members):
            gate = jnp.dot(x, wg_ref[m], preferred_element_type=F32)
            up = jnp.dot(x, wu_ref[m], preferred_element_type=F32)
            act = (gate / (1.0 + jnp.exp(-gate)) * up).astype(BF)
            acts.append(act)
        weights = [
            jnp.sum(jnp.where(lane == g_ref[0] * members + m, table, 0.0), axis=1, keepdims=True)
            for m in range(members)
        ]
        step = 512
        for at in range(0, features, step):
            total = jnp.zeros((count, step), F32)
            for m in range(members):
                total = total + weights[m] * jnp.dot(
                    acts[m], wd_ref[m, :, at : at + step], preferred_element_type=F32
                )
            o_ref[:, at : at + step] = total.astype(BF)

    return call(
        body,
        jax.ShapeDtypeStruct((count, features), BF),
        in_specs=[pl.BlockSpec(memory_space=pltpu.SMEM)]
        + [pl.BlockSpec(memory_space=pltpu.VMEM)] * 4,
        out_specs=pl.BlockSpec(memory_space=pltpu.VMEM),
    )(group, rows, w_gate, w_up, w_down)


def spread_sum(parts, table, groups, quads, pairs, tokens, slots):
    there, features = parts.shape
    here = quads * tokens

    def body(x_ref, t_ref, o_ref):
        hot = one_hot(t_ref[...], True, groups, quads, pairs, tokens, slots)
        o_ref[...] = jnp.dot(hot, x_ref[...], preferred_element_type=F32).astype(BF)

    return call(
        body,
        jax.ShapeDtypeStruct((here, features), BF),
        in_specs=[pl.BlockSpec(memory_space=pltpu.VMEM)] * 2,
        out_specs=pl.BlockSpec(memory_space=pltpu.VMEM),
    )(parts, table)


def finish_layer(parts, hidden):
    count, tokens, features = parts.shape

    def body(x_ref, h_ref, o_ref):
        total = h_ref[...].astype(F32)
        for s in range(count):
            total = total + x_ref[s].astype(F32)
        o_ref[...] = total.astype(BF)

    return call(
        body,
        jax.ShapeDtypeStruct((tokens, features), BF),
        in_specs=[pl.BlockSpec(memory_space=pltpu.VMEM)] * 2,
        out_specs=pl.BlockSpec(memory_space=pltpu.VMEM),
    )(parts, hidden)


def on_device(
    attn_heads, out_proj, residual_in, norm_gain, expert_ids, gate_weights, w_gate, w_up, w_down
):
    tokens, features = residual_in.shape
    groups, quads, pairs = (lax.axis_size(a) for a in ("group", "quad", "pair"))
    experts = groups * w_gate.shape[0]
    slots = 3 * tokens // 4
    near, far = ("group", "pair"), "quad"
    wide = features + LANES

    partial = project(attn_heads, out_proj, groups, quads, pairs, tokens)
    arrived = exchange(partial.reshape(groups * pairs, quads * tokens, features), near)
    summed = sum_blocks(arrived)
    arrived = exchange(summed.reshape(quads, tokens, features), far)
    hidden, sent = finish_hidden(
        arrived, residual_in, norm_gain.reshape(1, features), expert_ids, gate_weights, quads, experts
    )
    seen = exchange(sent, far).reshape(quads * tokens, wide)
    picked, table = pick_rows(seen, groups, quads, pairs, tokens, slots)
    rows = exchange(picked.reshape(groups * pairs, quads * slots, wide), near)
    group = lax.axis_index("group").astype(jnp.int32).reshape(1)
    blocks = experts_of(rows.reshape(-1, wide), w_gate, w_up, w_down, group)
    back = exchange(blocks.reshape(groups * pairs, quads * slots, features), near)
    mixed = spread_sum(back.reshape(-1, features), table, groups, quads, pairs, tokens, slots)
    arrived = exchange(mixed.reshape(quads, tokens, features), far)
    return finish_layer(arrived, hidden)


def solution(mesh):
    dp, groups, tensors = mesh.devices.shape
    split = Mesh(
        mesh.devices.reshape(dp, groups, tensors // 2, 2), ("dp", "group", "quad", "pair")
    )
    inner = ("group", "quad", "pair")
    rows = P(("dp", *inner), None)
    placed = (
        P("dp", inner),
        P(inner, None),
        rows,
        P(),
        rows,
        rows,
        P("group", None, ("quad", "pair")),
        P("group", None, ("quad", "pair")),
        P("group", ("quad", "pair"), None),
    )
    return jax.shard_map(
        on_device, mesh=split, in_specs=placed, out_specs=rows, check_vma=False
    )
```

time: 224 us -> 122 us (0.54)
  the two profiles are of different devices: /device:TPU:64 before, /device:TPU:896 now
where the time goes in v1:
time: 122 us
  blocking collectives  72.8 us (60%)
  waiting for transfers between devices  25.1 us (21%)
  starting transfers between devices  9.78 us (8%)
  Pallas kernels  7.2 us (6%)
  local copies, waits for them, and re-layouts  6.71 us (6%)
    all_to_all x4, blocking collectives, exchange(): return lax.all_to_all(blocks, axes, 0, 0, tiled=True)  72.8 us
    all_to_all x2, waiting for transfers between devices, exchange(): return lax.all_to_all(blocks, axes, 0, 0, tiled=True)  25.1 us
    all_to_all x2, starting transfers between devices, exchange(): return lax.all_to_all(blocks, axes, 0, 0, tiled=True)  9.78 us
    unnamed x22, local copies, waits for them, and re-layouts  6.7 us
  transfers between devices with their start and end apart: 2, of which 2 were waited for; matrix products, arithmetic and copies ran while one was open for 0% of the time, Pallas kernels for 0%

profile of v1, /device:TPU:896, one launch (start us, length us, event | category | flops | bytes accessed | tf_op | source)
XLA Modules:
  0.0 121.7 jit_solution(11681647552498097457)
XLA Ops:
  0.0 0.0 copy-start
  0.0 1.5 %copy-done = bf16[256,3584]{1,0:T(8,128)(2,1)S(1)} copy-done((bf16[256,3584]{1,0:T(8,128)(2,1)S(1)}, bf16[256,3584]{1,0:T(8,128)(2,1)}, u32[]{:S(2)}) %copy-start) | copy-done | bytes 1835032
  1.5 0.0 copy-start.5
  1.5 0.9 copy-done.5
  2.4 1.8 %shard_map.91 = bf16[256,3584]{1,0:T(8,128)(2,1)S(1)} custom-call(bf16[256,256]{1,0:T(8,128)(2,1)S(1)} %copy-done.5, bf16[256,3584]{1,0:T(8,128)(2,1)S(1)} %copy-done), custom_call_target="tpu_custom_call" | custom-call | tf_op jit(solution)/shard_map/pallas_call | solution.py:47
  4.2 29.5 %all_to_all.30.x_ref = bf16[8,32,3584]{2,1,0:T(8,128)(2,1)S(1)} all-to-all(bf16[8,32,3584]{2,1,0:T(8,128)(2,1)S(1)} %bitcast.9), channel_id=1, replica_groups=mesh['dp'=32,'group'=4,'quad'=4,'pair'=2] {'group','pair'}, dimensions={0} | all-to-all | bytes 3670016 | tf_op jit(solution)/shard_map/all_to_all | solution.py:30
  33.7 0.0 copy-start.7
  33.7 0.9 shard_map.92
  34.7 6.2 %all-to-all-start.1 = ((bf16[4,8,3584]{2,1,0:T(8,128)(2,1)}), bf16[4,8,3584]{2,1,0:T(8,128)(2,1)S(1)}, u32[]{:S(2)}, u32[]{:S(2)}) async-start(bf16[4,8,3584]{2,1,0:T(8,128)(2,1)} %bitcast.2), calls=%async_computation.1 | async-start | bytes 458752 | tf_op jit(solution)/shard_map/all_to_all | solution.py:30
  40.9 0.0 copy-done.7
  40.9 0.0 copy-done.8
  40.9 0.1 copy.10.id_ref
  41.0 0.0 copy-done.9
  41.0 0.1 copy.11.w_ref
  41.1 9.3 %all-to-all-done.1.x_ref = bf16[4,8,3584]{2,1,0:T(8,128)(2,1)S(1)} async-done(((bf16[4,8,3584]{2,1,0:T(8,128)(2,1)}), bf16[4,8,3584]{2,1,0:T(8,128)(2,1)S(1)}, u32[]{:S(2)}, u32[]{:S(2)}) %all-to-all-start.1) | async-done | bytes 229408 | tf_op jit(solution)/shard_map/all_to_all | solution.py:30
  50.4 0.0 copy-done.6
  50.4 0.2 shard_map.93
  50.5 0.0 copy-start.1
  50.6 12.1 %all_to_all.31 = bf16[4,8,3712]{2,1,0:T(8,128)(2,1)S(1)} all-to-all(bf16[4,8,3712]{2,1,0:T(8,128)(2,1)S(1)} %get-tuple-element.9), channel_id=1, replica_groups=mesh['dp'=32,'group'=4,'quad'=4,'pair'=2] {'quad'}, dimensions={0} | all-to-all | bytes 475136 | tf_op jit(solution)/shard_map/all_to_all | solution.py:30
  62.7 0.6 shard_map.94
  63.3 0.0 copy-start.4
  63.3 1.1 copy-done.4
  64.4 3.6 %all-to-all-start.3 = ((bf16[8,24,3712]{2,1,0:T(8,128)(2,1)}), bf16[8,24,3712]{2,1,0:T(8,128)(2,1)S(1)}, u32[]{:S(2)}, u32[]{:S(2)}) async-start(bf16[8,24,3712]{2,1,0:T(8,128)(2,1)} %bitcast.13), calls=%async_computation.3 | async-start | bytes 2850816 | tf_op jit(solution)/shard_map/all_to_all | solution.py:30
  68.0 15.8 %all-to-all-done.3 = bf16[8,24,3712]{2,1,0:T(8,128)(2,1)S(1)} async-done(((bf16[8,24,3712]{2,1,0:T(8,128)(2,1)}), bf16[8,24,3712]{2,1,0:T(8,128)(2,1)S(1)}, u32[]{:S(2)}, u32[]{:S(2)}) %all-to-all-start.3) | async-done | bytes 1425440 | tf_op jit(solution)/shard_map/all_to_all | solution.py:30
  83.8 0.0 copy-done.1
  83.8 1.5 %copy-done.2 = bf16[2,3584,128]{2,1,0:T(8,128)(2,1)S(1)} copy-done((bf16[2,3584,128]{2,1,0:T(8,128)(2,1)S(1)}, bf16[2,3584,128]{2,1,0:T(8,128)(2,1)}, u32[]{:S(2)}) %copy-start.2) | copy-done | bytes 1835032
  85.3 1.5 %copy-done.3 = bf16[2,128,3584]{2,1,0:T(8,128)(2,1)S(1)} copy-done((bf16[2,128,3584]{2,1,0:T(8,128)(2,1)S(1)}, bf16[2,128,3584]{2,1,0:T(8,128)(2,1)}, u32[]{:S(2)}) %copy-start.3) | copy-done | bytes 1835032
  86.8 2.3 %shard_map.95 = bf16[192,3584]{1,0:T(8,128)(2,1)S(1)} custom-call(s32[1]{0:T(128)} %bitcast.g_ref, bf16[192,3712]{1,0:T(8,128)(2,1)S(1)} %bitcast.10, bf16[2,3584,128]{2,1,0:T(8,128)(2,1)S(1)} %copy-done.1, bf16[2,3584,128]{2,1,0:T(8,128)(2,1)S(1)} %copy-done.2, bf16[2,128,3584]{2,1,0:T(8,128)(2,1)S(1)} %copy-done.3), custom_call_target="tpu_custom_call" | custom-call | tf_op jit(solution)/shard_map/pallas_call | solution.py:202
  89.2 19.5 %all_to_all.32 = bf16[8,24,3584]{2,1,0:T(8,128)(2,1)S(1)} all-to-all(bf16[8,24,3584]{2,1,0:T(8,128)(2,1)S(1)} %bitcast.12), channel_id=1, replica_groups=mesh['dp'=32,'group'=4,'quad'=4,'pair'=2] {'group','pair'}, dimensions={0} | all-to-all | bytes 2752512 | tf_op jit(solution)/shard_map/all_to_all | solution.py:30
  108.7 0.7 shard_map.96
  109.4 11.6 %all_to_all.33.x_ref = bf16[4,8,3584]{2,1,0:T(8,128)(2,1)S(1)} all-to-all(bf16[4,8,3584]{2,1,0:T(8,128)(2,1)S(1)} %bitcast.15), channel_id=1, replica_groups=mesh['dp'=32,'group'=4,'quad'=4,'pair'=2] {'quad'}, dimensions={0} | all-to-all | bytes 458752 | tf_op jit(solution)/shard_map/all_to_all | solution.py:30
  121.0 0.7 shard_map.97
  (6 shorter events, 0.0 us)
Async XLA Ops:
  0.0 1.5 %copy-start = (bf16[256,3584]{1,0:T(8,128)(2,1)S(1)}, bf16[256,3584]{1,0:T(8,128)(2,1)}, u32[]{:S(2)}) copy-start(bf16[256,3584]{1,0:T(8,128)(2,1)} %w_ref.2) | copy-start | bytes 5505028
  1.5 0.9 copy-start.5
  33.7 7.1 %copy-start.7 = (f32[3584]{0:T(1024)S(1)}, f32[3584]{0:T(1024)}, u32[]{:S(2)}) copy-start(f32[3584]{0:T(1024)} %param.12) | copy-start | bytes 43012
  33.7 7.2 %copy-start.8 = (s32[8,4]{0,1:T(4,128)S(1)}, s32[8,4]{0,1:T(4,128)}, u32[]{:S(2)}) copy-start(s32[8,4]{0,1:T(4,128)} %param.13) | copy-start | bytes 388
  33.7 7.2 %copy-start.9 = (bf16[8,4]{0,1:T(4,128)(2,1)S(1)}, bf16[8,4]{0,1:T(4,128)(2,1)}, u32[]{:S(2)}) copy-start(bf16[8,4]{0,1:T(4,128)(2,1)} %param.14) | copy-start | bytes 196
  33.7 16.6 %copy-start.6 = (bf16[8,3584]{1,0:T(8,128)(2,1)S(1)}, bf16[8,3584]{1,0:T(8,128)(2,1)}, u32[]{:S(2)}) copy-start(bf16[8,3584]{1,0:T(8,128)(2,1)} %r_ref.1) | copy-start | bytes 172036
  34.7 15.7 %all-to-all-start.1 = ((bf16[4,8,3584]{2,1,0:T(8,128)(2,1)}), bf16[4,8,3584]{2,1,0:T(8,128)(2,1)S(1)}, u32[]{:S(2)}, u32[]{:S(2)}) async-start(bf16[4,8,3584]{2,1,0:T(8,128)(2,1)} %bitcast.2), calls=%async_computation.1 | async-start | bytes 458752 | tf_op jit(solution)/shard_map/all_to_all | solution.py:30
  50.5 33.3 %copy-start.1 = (bf16[2,3584,128]{2,1,0:T(8,128)(2,1)S(1)}, bf16[2,3584,128]{2,1,0:T(8,128)(2,1)}, u32[]{:S(2)}) copy-start(bf16[2,3584,128]{2,1,0:T(8,128)(2,1)} %wg_ref.1) | copy-start | bytes 5505028
  63.3 1.1 copy-start.4
  64.4 19.4 %all-to-all-start.3 = ((bf16[8,24,3712]{2,1,0:T(8,128)(2,1)}), bf16[8,24,3712]{2,1,0:T(8,128)(2,1)S(1)}, u32[]{:S(2)}, u32[]{:S(2)}) async-start(bf16[8,24,3712]{2,1,0:T(8,128)(2,1)} %bitcast.13), calls=%async_computation.3 | async-start | bytes 2850816 | tf_op jit(solution)/shard_map/all_to_all | solution.py:30
  83.8 1.5 %copy-start.2 = (bf16[2,3584,128]{2,1,0:T(8,128)(2,1)S(1)}, bf16[2,3584,128]{2,1,0:T(8,128)(2,1)}, u32[]{:S(2)}) copy-start(bf16[2,3584,128]{2,1,0:T(8,128)(2,1)} %wu_ref.1) | copy-start | bytes 5505028
  85.3 1.5 %copy-start.3 = (bf16[2,128,3584]{2,1,0:T(8,128)(2,1)S(1)}, bf16[2,128,3584]{2,1,0:T(8,128)(2,1)}, u32[]{:S(2)}) copy-start(bf16[2,128,3584]{2,1,0:T(8,128)(2,1)} %wd_ref.1) | copy-start | bytes 5505028
